TPU v7x, 32 devices: a whole 2x2x4 slice. The times are simulated.
32 devices in a mesh: grp: 4 (over y, x), dev: 8 (over z, core).
Axes of the slice: x: 2, y: 2, z: 4, core: 2. Of those that a mesh axis runs over, the one named last changes fastest.
Arguments:
- raw: bfloat16 [128, 16, 4096], P(('grp', 'dev'))
- dark: bfloat16 [16, 4096], replicated, may hold values from 0.049804688 to 0.29882812
- basis: bfloat16 [8, 4096], replicated, may hold values from -3 to 3
- counts: int32 [128], P(('grp', 'dev')), may hold values from 1 to 16, as said below
- positions: int32 [128], replicated, may hold values from 0 to 127, as said below
Outputs:
- corrected: bfloat16 [128, 16, 4096], P(('grp', 'dev'))
- pooled: bfloat16 [4, 16, 1, 30720], P('grp', None, None, 'dev')
Inputs may be any that keep to these rules, and one draw needn't show every extreme that they name: `counts`: the first tile of every device (4 tiles in acquisition order) has all 16 planes. A permutation of the tile positions of the slide image. The 4 tiles of the device at grp index g and dev index d lie in 4 different bands, all at tile columns d * 4 to d * 4 + 3.
All inputs are finite; a program needn't handle non-finite values.
Results may differ from a plain program's by a relative error of at most 0.0046.
Values may be sent and summed in bfloat16 or wider, within the bound.
A program may use at most 128 MiB of HBM per device.

v0:
```python
import jax
import jax.numpy as jnp
from jax import lax
from jax.sharding import PartitionSpec as P

ROWS = 2
COLS = 2048
OVL = 128


def shifted(value, axis, steps):
    count = lax.axis_size(axis)
    first, last = (max(0, -steps), min(count, count - steps))
    return lax.ppermute(value, axis, [(source, source + steps) for source in range(first, last)])


def feather():
    column = jnp.arange(COLS, dtype=jnp.float32) + 0.5
    return jnp.minimum(1.0, jnp.minimum(column / OVL, (COLS - column) / OVL))


def pooling(tiles):
    count = tiles.shape[0]
    planes = tiles.shape[1]
    shaped = tiles.reshape(count, planes, ROWS, COLS) * feather()
    return jnp.sum(shaped.reshape(count, planes, ROWS // 2, 2, COLS // 2, 2), axis=(3, 5)) * 0.25


def per_device(raw, dark, basis, counts, positions):
    tile_count, planes, pixels = raw.shape
    groups = lax.axis_size("grp")
    columns = lax.axis_size("dev")
    band_size = columns * tile_count
    live = (jnp.arange(planes, dtype=jnp.int32)[None, :] < counts[:, None]).astype(jnp.float32)
    projected = jnp.einsum("kx,tpx->tkp", basis, raw, preferred_element_type=jnp.float32)
    local_proj = jnp.sum(projected * live[:, None, :], axis=0)
    ones_row = jnp.ones((pixels,), jnp.bfloat16)
    local_sum = jnp.sum(
        jnp.einsum("tpx,x->tp", raw, ones_row, preferred_element_type=jnp.float32) * live, axis=0
    )
    local_live = jnp.sum(live, axis=0)
    proj, total, alive = lax.psum((local_proj, local_sum, local_live), ("grp", "dev"))
    dark_f = dark.astype(jnp.float32)
    dark_proj = jnp.dot(basis, dark.T, preferred_element_type=jnp.float32)
    dark_sum = jnp.sum(dark_f, axis=1)
    coef = (proj - alive[None, :] * dark_proj) / (total - alive * dark_sum)[None, :]
    shade = jnp.dot(coef.T, basis.astype(jnp.float32), precision=lax.Precision.HIGHEST)
    inverse = jnp.exp(-shade)
    corrected = (
        (raw.astype(jnp.float32) - dark_f[None]) * inverse[None] * live[:, :, None]
    ).astype(jnp.bfloat16)
    here_grp = lax.axis_index("grp")
    here_dev = lax.axis_index("dev")
    layout = positions.reshape(groups, columns, tile_count)
    mine = lax.dynamic_index_in_dim(
        lax.dynamic_index_in_dim(layout, here_grp, 0, False), here_dev, 0, False
    )
    select = mine[None, :] // band_size == jnp.arange(groups, dtype=jnp.int32)[:, None]
    column_tiles = lax.dynamic_index_in_dim(layout, here_dev, 1, False)
    arrives = column_tiles // band_size == here_grp
    slot_of = jnp.sum(jnp.where(arrives, column_tiles % tile_count, 0), axis=1)
    place = slot_of[None, :] == jnp.arange(tile_count, dtype=jnp.int32)[:, None]
    own_cells = (
        pooling(corrected.astype(jnp.float32))
        .astype(jnp.bfloat16)
        .reshape(tile_count, planes, ROWS // 2 * (COLS // 2))
    )
    outgoing = jnp.einsum(
        "bs,spx->bpx", select.astype(jnp.bfloat16), own_cells, preferred_element_type=jnp.float32
    ).astype(jnp.bfloat16)
    arrived = lax.all_to_all(outgoing, "grp", split_axis=0, concat_axis=0, tiled=True)
    placed = jnp.einsum(
        "jb,bpx->jpx", place.astype(jnp.bfloat16), arrived, preferred_element_type=jnp.float32
    ).astype(jnp.bfloat16)
    cells = placed.reshape(tile_count, planes, ROWS // 2, COLS // 2)
    cells = lax.optimization_barrier(cells)
    half_step = (COLS - OVL) // 2
    half_ovl = OVL // 2
    head = cells[..., :half_step].astype(jnp.float32)
    tail = cells[..., half_step:]
    spill = shifted(tail[-1], "dev", 1)
    carried = jnp.concatenate([spill[None], tail[:-1]], axis=0)
    carried = jnp.pad(carried, ((0, 0), (0, 0), (0, 0), (0, half_step - half_ovl))).astype(
        jnp.float32
    )
    merged = head + carried
    result = jnp.transpose(merged, (1, 2, 0, 3)).reshape(
        1, planes, ROWS // 2, tile_count * half_step
    )
    return (corrected, result.astype(jnp.bfloat16))


def solution(mesh):
    in_specs = (P(("grp", "dev"), None, None), P(), P(), P(("grp", "dev")), P())
    out_specs = (P(("grp", "dev"), None, None), P("grp", None, None, "dev"))
    return jax.shard_map(
        per_device, mesh=mesh, in_specs=in_specs, out_specs=out_specs, check_vma=False
    )
```

profile of v0, /device:TPU:1, one launch (start us, length us, event | category | flops | bytes accessed | tf_op | source)
XLA Modules:
  0.0 94.8 jit_solution(9570556487243521192)
XLA Ops:
  0.6 1.1 %convert_reduce_fusion = f32[16]{0:T(128)S(1)} fusion(bf16[16,4096]{1,0:T(8,128)(2,1)} %param.6), kind=kLoop, calls=%fused_computation.22 | loop fusion | flops 131056 | bytes 131136 | tf_op jit(solution)/shard_map/reduce_sum | solution.py:45
  1.7 0.9 convert_element_type.62
  2.7 0.7 fusion.18
  3.4 1.7 %fusion.12 = f32[1,4,16]{2,0,1:T(1,128)S(1)} fusion(bf16[4,16,4096]{2,1,0:T(8,128)(2,1)} %param.5), kind=kOutput, calls=%fused_computation.23 | convolution fusion | flops 524288 | bytes 524544 | tf_op jit(solution)/shard_map/tpx,x->tp/dot_general | solution.py:39
  5.2 0.8 fusion.26
  5.9 1.8 %fusion.2 = f32[16,8]{0,1:T(8,128)S(1)} fusion(bf16[4,16,4096]{2,1,0:T(8,128)(2,1)} %param.5, bf16[8,4096]{1,0:T(8,128)(2,1)S(1)} %copy-done, f32[4,16]{1,0:T(4,128)S(1)} %fusion.18), kind=kOutput, calls=%fused_computation.7 | convolution fusion | flops 4195200 | bytes 590592 | tf_op jit(solution)/shard_map/kx,tpx->tkp/dot_general | solution.py:35
  7.7 40.5 %all-reduce.1 = (f32[8,16]{1,0:T(8,128)S(1)}, f32[16]{0:T(128)S(1)}, f32[16]{0:T(128)S(1)}) all-reduce(f32[8,16]{1,0:T(8,128)S(1)} %bitcast.39, f32[16]{0:T(128)S(1)} %get-tuple-element.3, f32[16]{0:T(128)S(1)} %get-tuple-element.2), channel_id=1, replica_groups=mesh['grp'=4,'dev'=8] {'grp','dev'}, use_global_device_ids=true, to_apply=%region_1.0 | all-reduce | flops 160 | bytes 1280 | tf_op jit(solution)/shard_map/psum | solution.py:42
  48.2 1.1 %fusion.4 = f32[8,16]{1,0:T(8,128)S(1)} fusion(f32[8,16]{1,0:T(8,128)S(1)} %get-tuple-element.4, bf16[8,4096]{1,0:T(8,128)(2,1)S(1)} %copy-done, bf16[16,4096]{1,0:T(8,128)(2,1)} %param.6, f32[16]{0:T(128)S(1)} %multiply_subtract_fusion, f32[16]{0:T(128)S(1)} %get-tuple-element.6), kind=kOutput, calls=%fused_computation.10 | convolution fusion | flops 1048960 | bytes 197760 | tf_op jit(solution)/shard_map/dot_general | solution.py:44
  49.3 0.3 fusion
  49.6 1.2 %multiply_convert_fusion = bf16[4,16,4096]{2,1,0:T(8,128)(2,1)S(1)} fusion(bf16[4,16,4096]{2,1,0:T(8,128)(2,1)} %param.5, f32[4,16]{1,0:T(4,128)S(1)} %fusion.18, f32[16,4096]{1,0:T(8,128)S(1)} %fusion, f32[16,4096]{1,0:T(8,128)S(1)} %convert_element_type.62), kind=kLoop, calls=%fused_computation.11 | loop fusion | flops 1310720 | bytes 1573120 | tf_op jit(solution)/shard_map/convert_element_type | solution.py:51
  50.9 4.1 %copy.17 = f32[4,16,4096]{1,2,0:T(8,128)} copy(bf16[4,16,4096]{2,1,0:T(8,128)(2,1)S(1)} %multiply_convert_fusion) | data formatting | bytes 1572864 | tf_op jit(solution)/shard_map/reshape | solution.py:25
  54.9 0.2 copy.18
  55.2 23.0 %multiply_reduce_fusion = f32[4,16,1024]{1,2,0:T(8,128)S(1)} fusion(f32[4,16,1,2,1024,2]{1,5,4,3,0,2:T(2,128)} %bitcast.38, f32[1024,2]{1,0:T(8,128)S(1)} %copy.18), kind=kLoop, calls=%fused_computation | loop fusion | flops 458752 | bytes 1318912 | tf_op jit(solution)/shard_map/reduce_sum | solution.py:26
  78.1 0.6 copy.19
  78.8 0.1 reshape.162
  78.9 0.2 convolution_convert_fusion.1
  79.1 0.7 copy.21
  79.8 3.3 %all-to-all-start = ((bf16[4,16,1024]{2,1,0:T(8,128)(2,1)}), bf16[4,16,1024]{2,1,0:T(8,128)(2,1)S(1)}, u32[]{:S(2)}, u32[]{:S(2)}) async-start(bf16[4,16,1024]{2,1,0:T(8,128)(2,1)} %copy.21), calls=%async_computation | async-start | bytes 262144 | tf_op jit(solution)/shard_map/all_to_all | solution.py:71
  83.1 0.1 fusion.17
  83.3 3.7 %all-to-all-done = bf16[4,16,1024]{2,1,0:T(8,128)(2,1)S(1)} async-done(((bf16[4,16,1024]{2,1,0:T(8,128)(2,1)}), bf16[4,16,1024]{2,1,0:T(8,128)(2,1)S(1)}, u32[]{:S(2)}, u32[]{:S(2)}) %all-to-all-start) | async-done | bytes 131104 | tf_op jit(solution)/shard_map/all_to_all | solution.py:71
  87.0 0.2 fusion.1
  87.3 5.9 %collective-permute-start = (bf16[16,1,64]{2,0,1:T(8,128)(2,1)S(1)}, bf16[16,1,64]{2,0,1:T(8,128)(2,1)S(1)}, u32[]{:S(2)}, u32[]{:S(2)}) collective-permute-start(bf16[16,1,64]{2,0,1:T(8,128)(2,1)S(1)} %bitcast.42), channel_id=1, source_target_pairs={{0,1},{1,2},{2,3},{3,4},{4,5},{5,6},{6,7},{8,9},{9,10},{10,11},{11... | collective-permute-start | bytes 6152 | tf_op jit(solution)/shard_map/ppermute | solution.py:14
  93.3 0.6 collective-permute-done
  94.0 0.8 convert_element_type.72
  (16 shorter events, 0.4 us)
Async XLA Ops:
  0.6 5.3 %copy-start = (bf16[8,4096]{1,0:T(8,128)(2,1)S(1)}, bf16[8,4096]{1,0:T(8,128)(2,1)}, u32[]{:S(2)}) copy-start(bf16[8,4096]{1,0:T(8,128)(2,1)} %param.7) | copy-start | bytes 196612
  50.9 27.3 %copy-start.1 = (bf16[4,16,4096]{2,1,0:T(8,128)(2,1)}, bf16[4,16,4096]{2,1,0:T(8,128)(2,1)S(1)}, u32[]{:S(2)}) copy-start(bf16[4,16,4096]{2,1,0:T(8,128)(2,1)S(1)} %multiply_convert_fusion) | copy-start | bytes 1572868
  54.9 23.8 %copy-start.2 = (s32[128]{0:T(128)S(1)}, s32[128]{0:T(128)}, u32[]{:S(2)}) copy-start(s32[128]{0:T(128)} %param.9) | copy-start | bytes 1540
  79.8 7.2 %all-to-all-start = ((bf16[4,16,1024]{2,1,0:T(8,128)(2,1)}), bf16[4,16,1024]{2,1,0:T(8,128)(2,1)S(1)}, u32[]{:S(2)}, u32[]{:S(2)}) async-start(bf16[4,16,1024]{2,1,0:T(8,128)(2,1)} %copy.21), calls=%async_computation | async-start | bytes 262144 | tf_op jit(solution)/shard_map/all_to_all | solution.py:71
  87.3 6.7 %collective-permute-start = (bf16[16,1,64]{2,0,1:T(8,128)(2,1)S(1)}, bf16[16,1,64]{2,0,1:T(8,128)(2,1)S(1)}, u32[]{:S(2)}, u32[]{:S(2)}) collective-permute-start(bf16[16,1,64]{2,0,1:T(8,128)(2,1)S(1)} %bitcast.42), channel_id=1, source_target_pairs={{0,1},{1,2},{2,3},{3,4},{4,5},{5,6},{6,7},{8,9},{9,10},{10,11},{11... | collective-permute-start | bytes 6152 | tf_op jit(solution)/shard_map/ppermute | solution.py:14
where the time goes:
time: 95.3 us; the launch traced here: 94.8 us
  blocking collectives  40.5 us (42%)
  other arithmetic  27.9 us (29%)
  starting transfers between devices  9.24 us (10%)
  local copies, waits for them, and re-layouts  6.65 us (7%)
  matrix products  5.32 us (6%)
  waiting for transfers between devices  4.34 us (5%)
    psum x1, blocking collectives, per_device(): lax.psum((local_proj, local_sum, local_live), ('grp', 'dev'))  40.5 us
    reduce_sum x1, other arithmetic, pooling(): jnp.sum(shaped.reshape(count, planes, ROWS // 2, 2, COLS // 2, 2), axis=(...  23 us
    ppermute x1, starting transfers between devices, shifted(): lax.ppermute(value, axis, [(source, source + steps) for source in range(f...  5.91 us
    reshape x1, local copies, waits for them, and re-layouts, pooling(): shaped = tiles.reshape(count, planes, ROWS, COLS) * feather()  4.06 us
    all_to_all x1, waiting for transfers between devices, per_device(): lax.all_to_all(outgoing, 'grp', split_axis=0, concat_axis=0, tiled=True)  3.7 us
    all_to_all x1, starting transfers between devices, per_device(): lax.all_to_all(outgoing, 'grp', split_axis=0, concat_axis=0, tiled=True)  3.32 us
  transfers between devices with their start and end apart: 2, of which 2 were waited for; matrix products, arithmetic and copies ran while one was open for 0% of the time, Pallas kernels for 0%

commit v1 on v0

--- a/solution.py
+++ b/solution.py
@@ -39,7 +39,7 @@
         jnp.einsum("tpx,x->tp", raw, ones_row, preferred_element_type=jnp.float32) * live, axis=0
     )
     local_live = jnp.sum(live, axis=0)
-    proj, total, alive = lax.psum((local_proj, local_sum, local_live), ("grp", "dev"))
+    proj, total, alive = lax.psum(lax.psum((local_proj, local_sum, local_live), "dev"), "grp")
     dark_f = dark.astype(jnp.float32)
     dark_proj = jnp.dot(basis, dark.T, preferred_element_type=jnp.float32)
     dark_sum = jnp.sum(dark_f, axis=1)

time: 95.3 us -> 79.8 us (0.84)
  blocking collectives: 40.5 us -> 22.9 us
  waiting for transfers between devices: 4.34 us -> 6.1 us
    psum x1 -> x2, blocking collectives: 40.5 us -> 22.9 us  [the longest x1 14.8 us: per_device(): lax.psum((local_proj, local_sum, local_live), 'dev')]
    ppermute x1, waiting for transfers between devices: 0.65 us -> 2.4 us  [shifted(): lax.ppermute(value, axis, [(source, source + steps) for source in range(f...]
where the time goes in v1:
time: 79.8 us; the launch traced here: 79.2 us
  other arithmetic  27.9 us (35%)
  blocking collectives  22.9 us (29%)
  starting transfers between devices  9.47 us (12%)
  local copies, waits for them, and re-layouts  6.65 us (8%)
  waiting for transfers between devices  6.1 us (8%)
  matrix products  5.32 us (7%)
  between operations  0.83 us (1%)
    reduce_sum x1, other arithmetic, pooling(): jnp.sum(shaped.reshape(count, planes, ROWS // 2, 2, COLS // 2, 2), axis=(...  23 us
    psum x1, blocking collectives, per_device(): lax.psum((local_proj, local_sum, local_live), 'dev')  14.8 us
    psum x1, blocking collectives, per_device(): lax.psum(lax.psum((local_proj, local_sum, local_live), 'dev'), 'grp')  8.03 us
    ppermute x1, starting transfers between devices, shifted(): lax.ppermute(value, axis, [(source, source + steps) for source in range(f...  6.15 us
    reshape x1, local copies, waits for them, and re-layouts, pooling(): shaped = tiles.reshape(count, planes, ROWS, COLS) * feather()  4.06 us
    all_to_all x1, waiting for transfers between devices, per_device(): lax.all_to_all(outgoing, 'grp', split_axis=0, concat_axis=0, tiled=True)  3.7 us
    all_to_all x1, starting transfers between devices, per_device(): lax.all_to_all(outgoing, 'grp', split_axis=0, concat_axis=0, tiled=True)  3.32 us
    ppermute x1, waiting for transfers between devices, shifted(): lax.ppermute(value, axis, [(source, source + steps) for source in range(f...  2.4 us
  transfers between devices with their start and end apart: 2, of which 2 were waited for; matrix products, arithmetic and copies ran while one was open for 0% of the time, Pallas kernels for 0%

profile of v1, /device:TPU:1, one launch (start us, length us, event | category | flops | bytes accessed | tf_op | source)
XLA Modules:
  0.0 79.2 jit_solution(17609673582990852897)
XLA Ops:
  0.6 1.1 %convert_reduce_fusion = f32[16]{0:T(128)S(1)} fusion(bf16[16,4096]{1,0:T(8,128)(2,1)} %param.6), kind=kLoop, calls=%fused_computation.22 | loop fusion | flops 131056 | bytes 131136 | tf_op jit(solution)/shard_map/reduce_sum | solution.py:45
  1.7 0.9 %convert_element_type.62 = f32[16,4096]{1,0:T(8,128)S(1)} convert(bf16[16,4096]{1,0:T(8,128)(2,1)} %param.6) | non-fusion elementwise | flops 65536 | bytes 393216 | tf_op jit(solution)/shard_map/convert_element_type | solution.py:43
  2.7 0.7 fusion.18
  3.4 1.7 %fusion.12 = f32[1,4,16]{2,0,1:T(1,128)S(1)} fusion(bf16[4,16,4096]{2,1,0:T(8,128)(2,1)} %param.5), kind=kOutput, calls=%fused_computation.23 | convolution fusion | flops 524288 | bytes 524544 | tf_op jit(solution)/shard_map/tpx,x->tp/dot_general | solution.py:39
  5.2 0.8 fusion.26
  5.9 1.8 %fusion.2 = f32[16,8]{0,1:T(8,128)S(1)} fusion(bf16[4,16,4096]{2,1,0:T(8,128)(2,1)} %param.5, bf16[8,4096]{1,0:T(8,128)(2,1)S(1)} %copy-done, f32[4,16]{1,0:T(4,128)S(1)} %fusion.18), kind=kOutput, calls=%fused_computation.7 | convolution fusion | flops 4195200 | bytes 590592 | tf_op jit(solution)/shard_map/kx,tpx->tkp/dot_general | solution.py:35
  7.7 14.8 %all-reduce.1 = (f32[8,16]{1,0:T(8,128)S(1)}, f32[16]{0:T(128)S(1)}, f32[16]{0:T(128)S(1)}) all-reduce(f32[8,16]{1,0:T(8,128)S(1)} %bitcast.39, f32[16]{0:T(128)S(1)} %get-tuple-element.3, f32[16]{0:T(128)S(1)} %get-tuple-element.2), channel_id=1, replica_groups=mesh['grp'=4,'dev'=8] {'dev'}, use_global_device_ids=true, to_apply=%region_1.0 | all-reduce | flops 160 | bytes 1280 | tf_op jit(solution)/shard_map/psum | solution.py:42
  22.5 8.0 %all-reduce.2 = (f32[8,16]{1,0:T(8,128)S(1)}, f32[16]{0:T(128)S(1)}, f32[16]{0:T(128)S(1)}) all-reduce(f32[8,16]{1,0:T(8,128)S(1)} %get-tuple-element.4, f32[16]{0:T(128)S(1)} %get-tuple-element.5, f32[16]{0:T(128)S(1)} %get-tuple-element.6), channel_id=1, replica_groups=mesh['grp'=4,'dev'=8] {'grp'}, use_global_device_ids=true, to_apply=%region_2.0 | all-reduce | flops 160 | bytes 1280 | tf_op jit(solution)/shard_map/psum | solution.py:42
  30.6 1.1 %fusion.4 = f32[8,16]{1,0:T(8,128)S(1)} fusion(f32[8,16]{1,0:T(8,128)S(1)} %get-tuple-element.7, bf16[8,4096]{1,0:T(8,128)(2,1)S(1)} %copy-done, bf16[16,4096]{1,0:T(8,128)(2,1)} %param.6, f32[16]{0:T(128)S(1)} %multiply_subtract_fusion, f32[16]{0:T(128)S(1)} %get-tuple-element.9), kind=kOutput, calls=%fused_computation.10 | convolution fusion | flops 1048960 | bytes 197760 | tf_op jit(solution)/shard_map/dot_general | solution.py:44
  31.6 0.3 fusion
  32.0 1.2 %multiply_convert_fusion = bf16[4,16,4096]{2,1,0:T(8,128)(2,1)S(1)} fusion(bf16[4,16,4096]{2,1,0:T(8,128)(2,1)} %param.5, f32[4,16]{1,0:T(4,128)S(1)} %fusion.18, f32[16,4096]{1,0:T(8,128)S(1)} %fusion, f32[16,4096]{1,0:T(8,128)S(1)} %convert_element_type.62), kind=kLoop, calls=%fused_computation.11 | loop fusion | flops 1310720 | bytes 1573120 | tf_op jit(solution)/shard_map/convert_element_type | solution.py:51
  33.2 4.1 %copy.17 = f32[4,16,4096]{1,2,0:T(8,128)} copy(bf16[4,16,4096]{2,1,0:T(8,128)(2,1)S(1)} %multiply_convert_fusion) | data formatting | bytes 1572864 | tf_op jit(solution)/shard_map/reshape | solution.py:25
  37.3 0.2 copy.18
  37.5 23.0 %multiply_reduce_fusion = f32[4,16,1024]{1,2,0:T(8,128)S(1)} fusion(f32[4,16,1,2,1024,2]{1,5,4,3,0,2:T(2,128)} %bitcast.38, f32[1024,2]{1,0:T(8,128)S(1)} %copy.18), kind=kLoop, calls=%fused_computation | loop fusion | flops 458752 | bytes 1318912 | tf_op jit(solution)/shard_map/reduce_sum | solution.py:26
  60.5 0.6 copy.19
  61.2 0.2 convolution_convert_fusion.1
  61.4 0.7 copy.21
  62.1 3.3 %all-to-all-start = ((bf16[4,16,1024]{2,1,0:T(8,128)(2,1)}), bf16[4,16,1024]{2,1,0:T(8,128)(2,1)S(1)}, u32[]{:S(2)}, u32[]{:S(2)}) async-start(bf16[4,16,1024]{2,1,0:T(8,128)(2,1)} %copy.21), calls=%async_computation | async-start | bytes 262144 | tf_op jit(solution)/shard_map/all_to_all | solution.py:71
  65.5 0.1 fusion.17
  65.6 3.7 %all-to-all-done = bf16[4,16,1024]{2,1,0:T(8,128)(2,1)S(1)} async-done(((bf16[4,16,1024]{2,1,0:T(8,128)(2,1)}), bf16[4,16,1024]{2,1,0:T(8,128)(2,1)S(1)}, u32[]{:S(2)}, u32[]{:S(2)}) %all-to-all-start) | async-done | bytes 131104 | tf_op jit(solution)/shard_map/all_to_all | solution.py:71
  69.3 0.2 fusion.1
  69.6 6.2 %collective-permute-start = (bf16[16,1,64]{2,0,1:T(8,128)(2,1)S(1)}, bf16[16,1,64]{2,0,1:T(8,128)(2,1)S(1)}, u32[]{:S(2)}, u32[]{:S(2)}) collective-permute-start(bf16[16,1,64]{2,0,1:T(8,128)(2,1)S(1)} %bitcast.42), channel_id=1, source_target_pairs={{0,1},{1,2},{2,3},{3,4},{4,5},{5,6},{6,7},{8,9},{9,10},{10,11},{11... | collective-permute-start | bytes 6152 | tf_op jit(solution)/shard_map/ppermute | solution.py:14
  75.8 2.4 %collective-permute-done = bf16[16,1,64]{2,0,1:T(8,128)(2,1)S(1)} collective-permute-done((bf16[16,1,64]{2,0,1:T(8,128)(2,1)S(1)}, bf16[16,1,64]{2,0,1:T(8,128)(2,1)S(1)}, u32[]{:S(2)}, u32[]{:S(2)}) %collective-permute-start) | collective-permute-done | bytes 2080 | tf_op jit(solution)/shard_map/ppermute | solution.py:14
  78.3 0.8 %convert_element_type.72 = bf16[1,16,1,3840]{3,1,2,0:T(8,128)(2,1)} reshape(bf16[16,1,4,960]{3,2,0,1:T(4,128)(2,1)S(1)} %fusion.7) | data formatting | bytes 245760 | tf_op jit(solution)/shard_map/convert_element_type | solution.py:90
  (17 shorter events, 0.4 us)
Async XLA Ops:
  0.6 5.3 %copy-start = (bf16[8,4096]{1,0:T(8,128)(2,1)S(1)}, bf16[8,4096]{1,0:T(8,128)(2,1)}, u32[]{:S(2)}) copy-start(bf16[8,4096]{1,0:T(8,128)(2,1)} %param.7) | copy-start | bytes 196612
  33.2 27.3 %copy-start.1 = (bf16[4,16,4096]{2,1,0:T(8,128)(2,1)}, bf16[4,16,4096]{2,1,0:T(8,128)(2,1)S(1)}, u32[]{:S(2)}) copy-start(bf16[4,16,4096]{2,1,0:T(8,128)(2,1)S(1)} %multiply_convert_fusion) | copy-start | bytes 1572868
  37.3 23.8 %copy-start.2 = (s32[128]{0:T(128)S(1)}, s32[128]{0:T(128)}, u32[]{:S(2)}) copy-start(s32[128]{0:T(128)} %param.9) | copy-start | bytes 1540
  62.1 7.2 %all-to-all-start = ((bf16[4,16,1024]{2,1,0:T(8,128)(2,1)}), bf16[4,16,1024]{2,1,0:T(8,128)(2,1)S(1)}, u32[]{:S(2)}, u32[]{:S(2)}) async-start(bf16[4,16,1024]{2,1,0:T(8,128)(2,1)} %copy.21), calls=%async_computation | async-start | bytes 262144 | tf_op jit(solution)/shard_map/all_to_all | solution.py:71
  69.6 8.6 %collective-permute-start = (bf16[16,1,64]{2,0,1:T(8,128)(2,1)S(1)}, bf16[16,1,64]{2,0,1:T(8,128)(2,1)S(1)}, u32[]{:S(2)}, u32[]{:S(2)}) collective-permute-start(bf16[16,1,64]{2,0,1:T(8,128)(2,1)S(1)} %bitcast.42), channel_id=1, source_target_pairs={{0,1},{1,2},{2,3},{3,4},{4,5},{5,6},{6,7},{8,9},{9,10},{10,11},{11... | collective-permute-start | bytes 6152 | tf_op jit(solution)/shard_map/ppermute | solution.py:14
